TPU v7x, 128 devices: a whole 4x4x4 slice. The times are simulated.
128 devices in a mesh: dp: 32 (over x, z, core), rep: 4 (over y).
Axes of the slice: x: 4, y: 4, z: 4, core: 2. Of those that a mesh axis runs over, the one named last changes fastest.
Arguments:
- cross_in: bfloat16 [65536, 3456], P(('dp', 'rep')), may hold values from -24 to 24
- cotangent: bfloat16 [65536, 3456], P(('dp', 'rep')), may hold values from -24 to 24
- weight_down: bfloat16 [3456, 512], replicated, may hold values from -0.109375 to 0.109375
- weight_up: bfloat16 [512, 3456], replicated, may hold values from -0.25 to 0.25
- cross_bias: float32 [3456], replicated, may hold values from -3 to 3
- row_place: int32 [65536, 26], P(('dp', 'rep')), may hold values from 0 to 66559, as said below
- frequent_table: float32 [1024, 128], replicated, may hold values from -0.6 to 0.6
- frequent_accum: float32 [1024], replicated, may hold values from 416 to 106496
- shard_table: float32 [65536, 128], P('dp'), may hold values from -0.6 to 0.6
- shard_accum: float32 [65536], P('dp'), may hold values from 0.01 to 1
Outputs:
- new_frequent: float32 [1024, 128], replicated
- new_frequent_accum: float32 [1024], replicated
- new_shard: float32 [65536, 128], P('dp')
- new_shard_accum: float32 [65536], P('dp')
- grad_up: float32 [512, 3456], P(('dp', 'rep'))
- grad_down: float32 [3456, 512], P(('dp', 'rep'))
- grad_bias: float32 [3456], P(('dp', 'rep'))
Inputs may be any that keep to these rules, and one draw needn't show every extreme that they name: `row_place`: within the rows of one device (aligned blocks of 512 samples), at most 208 entries name rows of any one owner, and in every block some owner is named by exactly 208 entries; every owner is named at least once in every block.
All inputs are finite; a program needn't handle non-finite values.
Results may differ from a plain program's by a relative error of at most 0.0013.
The roundings to bfloat16 on the way count: a program that leaves them out, or rounds other values in their place, can miss the bound.
Values sent between devices are 32-bit elements; how exact they have to be, the bound alone decides.
A program may use at most 192 MiB of HBM per device.

v0:
```python
import jax
import jax.numpy as jnp
from jax import lax
from jax.sharding import PartitionSpec as P

learn_rate = 0.05
eps_ada = 1e-08


def row_adagrad(table, accum, grad):
    accum_new = accum + jnp.mean(grad * grad, axis=1)
    return (table - learn_rate * grad / (jnp.sqrt(accum_new)[:, None] + eps_ada), accum_new)


def body(
    cross_in,
    cotangent,
    weight_down,
    weight_up,
    cross_bias,
    row_place,
    frequent_table,
    frequent_accum,
    shard_table,
    shard_accum,
):
    emb_width = frequent_table.shape[1]
    num_tables = row_place.shape[1]
    local_rows = cross_in.shape[0]
    f_count = frequent_table.shape[0]
    owned_rows = shard_table.shape[0]
    hidden = jnp.dot(cross_in, weight_down, preferred_element_type=jnp.float32).astype(jnp.bfloat16)
    scaled = jnp.dot(hidden, weight_up, preferred_element_type=jnp.float32) + cross_bias
    cot_wide = cotangent.astype(jnp.float32)
    inner = cot_wide * cross_in.astype(jnp.float32)
    inner_half = inner.astype(jnp.bfloat16)
    back_low = lax.dot_general(
        inner_half, weight_up, (((1,), (1,)), ((), ())), preferred_element_type=jnp.float32
    ).astype(jnp.bfloat16)
    back_in = cot_wide * (scaled + 1.0) + lax.dot_general(
        back_low, weight_down, (((1,), (1,)), ((), ())), preferred_element_type=jnp.float32
    )
    local_up = lax.dot_general(
        hidden, inner_half, (((0,), (0,)), ((), ())), preferred_element_type=jnp.float32
    )
    local_down = lax.dot_general(
        cross_in, back_low, (((0,), (0,)), ((), ())), preferred_element_type=jnp.float32
    )
    local_bias = jnp.sum(inner, axis=0)
    grad_up, grad_down, grad_bias = (
        lax.psum_scatter(local_up, ("dp", "rep"), scatter_dimension=0, tiled=True),
        lax.psum_scatter(local_down, ("dp", "rep"), scatter_dimension=0, tiled=True),
        lax.psum_scatter(local_bias, ("dp", "rep"), scatter_dimension=0, tiled=True),
    )
    values = back_in[:, emb_width:].reshape(local_rows * num_tables, emb_width)
    places = row_place.reshape(-1)
    is_frequent = places < f_count
    freq_grad = jax.ops.segment_sum(values, jnp.where(is_frequent, places, f_count), f_count + 1)[
        :f_count
    ]
    shards = lax.axis_size("dp")
    capacity = local_rows * num_tables // (2 * shards)
    owners = jnp.where(is_frequent, shards, (places - f_count) // owned_rows)
    owner_row = jnp.where(is_frequent, 0, (places - f_count) % owned_rows)
    sorted_order = jnp.argsort(owners, stable=True)
    sorted_owner = owners[sorted_order]
    counts = jnp.sum((owners[:, None] == jnp.arange(shards + 1)[None, :]).astype(jnp.int32), axis=0)
    starts = jnp.cumsum(counts) - counts
    slot_pos = jnp.arange(owners.shape[0]) - starts[sorted_owner]
    target = jnp.where(sorted_owner < shards, sorted_owner * capacity + slot_pos, shards * capacity)
    bucket = (
        jnp.zeros((shards * capacity + 1, emb_width), jnp.float32)
        .at[target]
        .set(values[sorted_order])
    )
    bucket = bucket[: shards * capacity].reshape(shards, capacity, emb_width)
    bucket_rows = (
        jnp.zeros((shards * capacity + 1,), jnp.int32).at[target].set(owner_row[sorted_order])
    )
    bucket_rows = bucket_rows[: shards * capacity].reshape(shards, capacity)
    arrived, arrived_rows = (
        lax.all_to_all(bucket, "dp", split_axis=0, concat_axis=0, tiled=True),
        lax.all_to_all(bucket_rows, "dp", split_axis=0, concat_axis=0, tiled=True),
    )
    shard_grad = jax.ops.segment_sum(
        arrived.reshape(-1, emb_width), arrived_rows.reshape(-1), owned_rows
    )
    shard_grad = lax.psum(shard_grad, "rep")
    new_shard, new_shard_accum = row_adagrad(shard_table, shard_accum, shard_grad)
    freq_total = lax.psum(freq_grad, ("dp", "rep"))
    new_frequent, new_frequent_accum = row_adagrad(frequent_table, frequent_accum, freq_total)
    return (
        new_frequent,
        new_frequent_accum,
        new_shard,
        new_shard_accum,
        grad_up,
        grad_down,
        grad_bias,
    )


def solution(mesh):
    in_specs = (
        P(("dp", "rep"), None),
        P(("dp", "rep"), None),
        P(),
        P(),
        P(),
        P(("dp", "rep"), None),
        P(),
        P(),
        P("dp", None),
        P("dp"),
    )
    out_specs = (
        P(),
        P(),
        P("dp", None),
        P("dp"),
        P(("dp", "rep"), None),
        P(("dp", "rep"), None),
        P(("dp", "rep")),
    )
    return jax.shard_map(body, mesh=mesh, in_specs=in_specs, out_specs=out_specs, check_vma=False)
```

profile of v0, /device:TPU:1, one launch (start us, length us, event | category | flops | bytes accessed | tf_op | source)
XLA Modules:
  0.0 876.3 jit_solution(13880018079292635862)
XLA Ops:
  7.2 1.6 broadcast_add_fusion
  9.7 1.7 copy.31
  11.3 1.8 sub.33
  14.9 1.5 fusion.18
  18.1 1.4 reduce-window.9
  22.4 9.1 %sort.17 = (s32[13312]{0:T(1024)}, s32[13312]{0:T(1024)}) sort(s32[13312]{0:T(1024)} %copy-done.2, s32[13312]{0:T(1024)} %iota.12), dimensions={0}, to_apply=%region_3.0 | sort | flops 186368 | bytes 212992 | tf_op jit(solution)/shard_map/jit(argsort)/sort | solution.py:65
  31.5 1.4 fusion.19
  32.9 121.2 %gather_fusion = s32[13312]{0:T(1024)} fusion(s32[13312]{0:T(1024)} %copy-done.2, s32[13312]{0:T(1024)} %fusion.19), kind=kCustom, calls=%fused_computation | custom fusion | bytes 159744 | tf_op jit(solution)/shard_map/gather | solution.py:66
  154.1 5.3 compare_select_fusion.3
  159.4 4.2 compare_reduce_fusion.25
  163.7 16.6 %select_select_fusion = s32[13312]{0:T(1024)S(1)} fusion(pred[13312]{0:T(1024)(128)(4,1)S(1)} %get-tuple-element.62, pred[13312]{0:T(1024)(128)(4,1)S(1)} %get-tuple-element.61, pred[13312]{0:T(1024)(128)(4,1)S(1)} %get-tuple-element.60, pred[13312]{0:T(1024)(128)(4,1)S(1)} %get-tuple-element.59, pred[13312]{0:T(1024)(128)(4,1)S(1)} %get-tuple-element.58, ...), kind=kLoop, calls=%fused_computation.77 | loop fusion | flops 346112 | bytes 452712 | tf_op jit(solution)/shard_map/gather | solution.py:69
  180.3 1.6 compare_select_fusion
  181.8 120.7 %gather_fusion.1 = s32[13312]{0:T(1024)} fusion(s32[13312]{0:T(1024)} %get-tuple-element.72, s32[13312]{0:T(1024)} %fusion.19), kind=kCustom, calls=%fused_computation.1 | custom fusion | bytes 159744 | tf_op jit(solution)/shard_map/gather | solution.py:78
  302.6 49.8 %scatter_custom_fusion.1 = s32[6657]{0:T(1024)} fusion(s32[13312]{0:T(1024)} %bitcast.62, s32[13312]{0:T(1024)} %gather_fusion.1, s32[]{:T(128)} %constant.29.clone.1), kind=kCustom, calls=%fused_computation.83 | custom fusion | bytes 27140 | tf_op jit(solution)/shard_map/scatter | solution.py:78
  352.4 1.5 all_to_all.9
  353.9 9.8 %all-to-all-start = ((s32[32,1,208]{2,1,0:T(1,128)}), s32[32,1,208]{2,1,0:T(1,128)}, u32[]{:S(2)}, u32[]{:S(2)}) async-start(s32[32,1,208]{2,1,0:T(1,128)} %all_to_all.9), calls=%async_computation | async-start | bytes 65536 | tf_op jit(solution)/shard_map/all_to_all | solution.py:83
  363.7 2.6 convert_element_type.18
  367.9 2.0 convolution_convert_fusion
  369.9 2.1 fusion.10
  372.1 2.1 fusion.26
  374.3 2.1 fusion.27
  376.4 3.3 slice_add_fusion
  379.7 7.8 reshape.231
  387.5 108.6 %scatter_custom_fusion.2 = f32[6657,128]{1,0:T(8,128)S(1)} fusion(s32[13312]{0:T(1024)} %bitcast.63, f32[13312,128]{1,0:T(8,128)} %reshape.231, s32[13312]{0:T(1024)} %fusion.19, f32[]{:T(128)} %constant.21.clone.1), kind=kCustom, calls=%fused_computation.12 | custom fusion | bytes 3408896 | tf_op jit(solution)/shard_map/scatter | solution.py:74
  496.1 2.1 slice.62
  498.2 7.8 all-to-all-start.1
  506.1 1.7 copy.29
  507.8 1.8 reshape.157
  509.6 1.5 compare_select_fusion.2
  511.1 72.4 %scatter_custom_fusion = f32[1025,128]{1,0:T(8,128)} fusion(s32[13312]{0:T(1024)} %bitcast.64, f32[13312,128]{1,0:T(8,128)} %reshape.231, f32[]{:T(128)} %constant.21.clone.1), kind=kCustom, calls=%fused_computation.33 | custom fusion | flops 1703936 | bytes 525312 | tf_op jit(solution)/shard_map/scatter-add | solution.py:58
  583.4 1.9 slice.60
  585.3 1.4 reduce.27
  586.8 1.5 reshape.253
  588.2 41.0 %scatter_custom_fusion.3 = f32[2048,128]{1,0:T(8,128)} fusion(s32[6656]{0:T(1024)} %reshape.253, f32[6656,128]{1,0:T(8,128)} %bitcast.40, f32[]{:T(128)} %constant.21.clone.1), kind=kCustom, calls=%fused_computation.26 | custom fusion | flops 851968 | bytes 1049088 | tf_op jit(solution)/shard_map/scatter-add | solution.py:85
  629.4 6.2 convolution_bitcast_fusion
  635.6 5.1 fusion.6
  640.7 4.2 fusion.3
  644.8 67.5 %all-reduce.2 = f32[3456]{0:T(1024)} all-reduce(f32[3456]{0:T(1024)S(1)} %fusion.3), channel_id=4, replica_groups=mesh['dp'=32,'rep'=4] {'dp','rep'}, use_global_device_ids=true, to_apply=%region_14.15.clone | all-reduce | flops 3456 | bytes 27648
  712.3 1.3 dynamic-slice.2
  713.6 1.6 multiply_reduce_fusion
  715.2 1.3 sqrt_add_fusion
  716.5 3.0 divide_subtract_fusion
  719.4 140.0 %all-reduce.9.cloned.1.call-done = (f32[1024,128]{1,0:T(8,128)}, f32[512,3456]{1,0:T(8,128)}, f32[3456,512]{0,1:T(8,128)}) async-done(((f32[1024,128]{1,0:T(8,128)}, f32[512,3456]{1,0:T(8,128)}, f32[3456,512]{0,1:T(8,128)}), (f32[1024,128]{1,0:T(8,128)}, f32[512,3456]{1,0:T(8,128)}, f32[3456,512]{0,1:T(8,128)})) %all-reduce.9.cloned.1.call-update) | async-done | bytes 14680080 | tf_op jit(solution)/shard_map/psum | solution.py:90
  860.7 1.9 constant_dynamic-slice_fusion
  862.6 1.7 copy.33
  864.3 1.3 sqrt_add_fusion.1
  865.5 2.2 divide_subtract_fusion.1
  867.7 1.5 constant_dynamic-slice_fusion.1
  (45 shorter events, 10.3 us)
Async XLA Ops:
  7.2 362.8 %copy-start = (bf16[512,3456]{1,0:T(8,128)(2,1)S(1)}, bf16[512,3456]{1,0:T(8,128)(2,1)}, u32[]{:S(2)}) copy-start(bf16[512,3456]{1,0:T(8,128)(2,1)} %param.13) | copy-start | bytes 10616836
  16.4 0.6 copy-start.2
  353.9 144.3 %all-to-all-start = ((s32[32,1,208]{2,1,0:T(1,128)}), s32[32,1,208]{2,1,0:T(1,128)}, u32[]{:S(2)}, u32[]{:S(2)}) async-start(s32[32,1,208]{2,1,0:T(1,128)} %all_to_all.9), calls=%async_computation | async-start | bytes 65536 | tf_op jit(solution)/shard_map/all_to_all | solution.py:83
  363.7 3.1 copy-start.3
  363.7 4.1 copy-start.7
  367.9 2.1 copy-start.5
  369.9 2.1 copy-start.9
  372.1 4.3 copy-start.11
  372.1 2.2 copy-start.8
  374.3 2.1 copy-start.12
  498.2 131.1 %copy-start.4 = (bf16[512,3456]{1,0:T(8,128)(2,1)S(1)}, bf16[512,3456]{1,0:T(8,128)(2,1)}, u32[]{:S(2)}) copy-start(bf16[512,3456]{1,0:T(8,128)(2,1)} %param.10) | copy-start | bytes 10616836
  498.2 90.0 %all-to-all-start.1 = ((f32[32,208,128]{2,1,0:T(8,128)}), f32[32,208,128]{2,1,0:T(8,128)}, u32[]{:S(2)}, u32[]{:S(2)}) async-start(f32[32,208,128]{2,1,0:T(8,128)} %bitcast.56), calls=%async_computation.1 | async-start | bytes 6815744 | tf_op jit(solution)/shard_map/all_to_all | solution.py:82
  506.1 207.5 %all-reduce.7.cloned.1.call-start = ((), (), s32[]{:S(2)}) async-start(), calls=%async_computation.2 | async-start | bytes 2097152 | tf_op jit(solution)/shard_map/psum | solution.py:88
  629.3 230.1 %all-reduce.9.cloned.1.call-start = ((), (), s32[]{:S(2)}) async-start(), calls=%async_computation.3 | async-start | bytes 29360128 | tf_op jit(solution)/shard_map/psum | solution.py:90
  629.3 6.2 copy-start.6
  629.4 6.2 copy-start.10
  640.7 228.6 %copy-start.1 = (bf16[512,3456]{1,0:T(8,128)(2,1)S(1)}, bf16[512,3456]{1,0:T(8,128)(2,1)}, u32[]{:S(2)}) copy-start(bf16[512,3456]{1,0:T(8,128)(2,1)} %param.13) | copy-start | bytes 10616836
Sparse Core Ops, SparseCore 0:
  629.4 46.4 all-reduce.6
  683.0 176.4 all-reduce.8
where the time goes:
time: 884 us; the launch traced here: 876 us
  local copies, waits for them, and re-layouts  435 us (49%)
  other arithmetic  182 us (21%)
  waiting for transfers between devices  140 us (16%)
  blocking collectives  67.5 us (8%)
  matrix products  19.6 us (2%)
  starting transfers between devices  17.8 us (2%)
  between operations  14.5 us (2%)
    psum x1, waiting for transfers between devices, body(): freq_total = lax.psum(freq_grad, ('dp', 'rep'))  140 us
    gather x1, local copies, waits for them, and re-layouts, body(): sorted_owner = owners[sorted_order]  121 us
    gather x1, local copies, waits for them, and re-layouts, body(): owner_row[sorted_order]  121 us
    scatter x1, local copies, waits for them, and re-layouts, body(): bucket = jnp.zeros((shards * capacity + 1, emb_width), jnp.float32).at[ta...  109 us
    scatter-add x1, other arithmetic, body(): jax.ops.segment_sum(values, jnp.where(is_frequent, places, f_count), f_co...  72.4 us
    unnamed x1, blocking collectives  67.5 us
    scatter x1, local copies, waits for them, and re-layouts, body(): jnp.zeros((shards * capacity + 1,), jnp.int32).at[target]  49.8 us
    scatter-add x1, other arithmetic, body(): jax.ops.segment_sum(arrived.reshape(-1, emb_width), arrived_rows.reshape(...  41 us
  transfers between devices with their start and end apart: 4, of which 1 were waited for; matrix products, arithmetic and copies ran while one was open for 27% of the time, Pallas kernels for 0%

commit v1 on v0

--- a/solution.py
+++ b/solution.py
@@ -87,7 +87,8 @@
     )
     shard_grad = lax.psum(shard_grad, "rep")
     new_shard, new_shard_accum = row_adagrad(shard_table, shard_accum, shard_grad)
-    freq_total = lax.psum(freq_grad, ("dp", "rep"))
+    shards_2 = lax.all_gather(freq_grad, ("dp", "rep"))
+    freq_total = jnp.sum(shards_2, axis=0)
     new_frequent, new_frequent_accum = row_adagrad(frequent_table, frequent_accum, freq_total)
     return (
         new_frequent,

time: 884 us -> 1030 us (1.17)
  waiting for transfers between devices: 140 us -> 262 us
  other arithmetic: 182 us -> 202 us
    all_gather x0 -> x1, waiting for transfers between devices: none -> 163 us  [body(): shards_2 = lax.all_gather(freq_grad, ('dp', 'rep'))]
    psum x1 -> x0, waiting for transfers between devices: 140 us -> none  [body(): freq_total = lax.psum(freq_grad, ('dp', 'rep'))]
    unnamed x2 -> x4, waiting for transfers between devices: 0.03 us -> 59.2 us
    all_to_all x1, waiting for transfers between devices: 0.01 us -> 39.8 us  [body(): lax.all_to_all(bucket, 'dp', split_axis=0, concat_axis=0, tiled=True)]
    reduce_sum x0 -> x1, other arithmetic: none -> 21.8 us  [body(): freq_total = jnp.sum(shards_2, axis=0)]
  transfers between devices with their start and end apart: 4 -> 5, of which waited for: 1 -> 3; matrix products, arithmetic and copies ran while one was open for 27% -> 24% of each run, Pallas kernels for 0% -> 0%
where the time goes in v1:
time: 1030 us; the launch traced here: 1020 us
  local copies, waits for them, and re-layouts  436 us (42%)
  waiting for transfers between devices  262 us (25%)
  other arithmetic  202 us (20%)
  blocking collectives  66.6 us (6%)
  matrix products  19.7 us (2%)
  starting transfers between devices  17.6 us (2%)
  between operations  14.2 us (1%)
    all_gather x1, waiting for transfers between devices, body(): shards_2 = lax.all_gather(freq_grad, ('dp', 'rep'))  163 us
    gather x1, local copies, waits for them, and re-layouts, body(): sorted_owner = owners[sorted_order]  121 us
    gather x1, local copies, waits for them, and re-layouts, body(): owner_row[sorted_order]  121 us
    scatter x1, local copies, waits for them, and re-layouts, body(): bucket = jnp.zeros((shards * capacity + 1, emb_width), jnp.float32).at[ta...  110 us
    scatter-add x1, other arithmetic, body(): jax.ops.segment_sum(values, jnp.where(is_frequent, places, f_count), f_co...  72.2 us
    unnamed x1, blocking collectives  66.6 us
    unnamed x4, waiting for transfers between devices  59.2 us
    scatter x1, local copies, waits for them, and re-layouts, body(): jnp.zeros((shards * capacity + 1,), jnp.int32).at[target]  49.8 us
  transfers between devices with their start and end apart: 5, of which 3 were waited for; matrix products, arithmetic and copies ran while one was open for 24% of the time, Pallas kernels for 0%

profile of v1, /device:TPU:1, one launch (start us, length us, event | category | flops | bytes accessed | tf_op | source)
XLA Modules:
  0.0 1018.0 jit_solution(5747077863481671862)
XLA Ops:
  7.2 1.6 broadcast_add_fusion
  9.7 1.7 copy.31
  11.3 1.8 sub.33
  14.9 1.5 fusion.18
  18.1 1.4 reduce-window.9
  22.4 9.1 sort.17
  31.5 1.4 fusion.19
  32.9 121.2 %gather_fusion = s32[13312]{0:T(1024)} fusion(s32[13312]{0:T(1024)} %copy-done.2, s32[13312]{0:T(1024)} %fusion.19), kind=kCustom, calls=%fused_computation | custom fusion | bytes 159744 | tf_op jit(solution)/shard_map/gather | solution.py:66
  154.1 5.3 compare_select_fusion.3
  159.4 4.2 compare_reduce_fusion.25
  163.7 16.6 %select_select_fusion = s32[13312]{0:T(1024)S(1)} fusion(pred[13312]{0:T(1024)(128)(4,1)S(1)} %get-tuple-element.62, pred[13312]{0:T(1024)(128)(4,1)S(1)} %get-tuple-element.61, pred[13312]{0:T(1024)(128)(4,1)S(1)} %get-tuple-element.60, pred[13312]{0:T(1024)(128)(4,1)S(1)} %get-tuple-element.59, pred[13312]{0:T(1024)(128)(4,1)S(1)} %get-tuple-element.58, ...), kind=kLoop, calls=%fused_computation.77 | loop fusion | flops 346112 | bytes 452712 | tf_op jit(solution)/shard_map/gather | solution.py:69
  180.3 1.6 compare_select_fusion
  181.8 120.7 %gather_fusion.1 = s32[13312]{0:T(1024)} fusion(s32[13312]{0:T(1024)} %get-tuple-element.71, s32[13312]{0:T(1024)} %fusion.19), kind=kCustom, calls=%fused_computation.1 | custom fusion | bytes 159744 | tf_op jit(solution)/shard_map/gather | solution.py:78
  302.6 49.8 %scatter_custom_fusion.1 = s32[6657]{0:T(1024)} fusion(s32[13312]{0:T(1024)} %bitcast.63, s32[13312]{0:T(1024)} %gather_fusion.1, s32[]{:T(128)} %constant.29.clone.1), kind=kCustom, calls=%fused_computation.83 | custom fusion | bytes 27140 | tf_op jit(solution)/shard_map/scatter | solution.py:78
  352.4 1.5 all_to_all.9
  353.9 9.8 all-to-all-start
  363.7 2.6 convert_element_type.18
  367.9 2.1 convolution_convert_fusion
  370.0 2.2 fusion.10
  372.2 2.1 fusion.26
  374.3 2.1 fusion.27
  376.5 3.3 slice_add_fusion
  379.8 7.8 reshape.231
  387.6 109.8 %scatter_custom_fusion.2 = f32[6657,128]{1,0:T(8,128)} fusion(s32[13312]{0:T(1024)} %bitcast.64, f32[13312,128]{1,0:T(8,128)} %reshape.231, s32[13312]{0:T(1024)} %fusion.19, f32[]{:T(128)} %constant.21.clone.1), kind=kCustom, calls=%fused_computation.12 | custom fusion | bytes 3408896 | tf_op jit(solution)/shard_map/scatter | solution.py:74
  497.4 4.2 slice.62
  501.5 7.6 all-to-all-start.1
  509.2 1.5 reduce.27
  510.6 1.5 reshape.253
  512.1 39.8 %all-to-all-done.1 = f32[32,208,128]{2,1,0:T(8,128)} async-done(((f32[32,208,128]{2,1,0:T(8,128)}), f32[32,208,128]{2,1,0:T(8,128)}, u32[]{:S(2)}, u32[]{:S(2)}) %all-to-all-start.1) | async-done | bytes 3407904 | tf_op jit(solution)/shard_map/all_to_all | solution.py:82
  551.8 41.2 %scatter_custom_fusion.3 = f32[2048,128]{1,0:T(8,128)} fusion(s32[6656]{0:T(1024)} %reshape.253, f32[6656,128]{1,0:T(8,128)} %bitcast.41, f32[]{:T(128)} %constant.21.clone.1), kind=kCustom, calls=%fused_computation.26 | custom fusion | flops 851968 | bytes 1049088 | tf_op jit(solution)/shard_map/scatter-add | solution.py:85
  593.2 6.2 convolution_bitcast_fusion
  599.4 5.0 fusion.6
  604.5 1.7 copy.29
  606.1 1.8 reshape.157
  608.0 1.5 compare_select_fusion.2
  609.4 72.2 %scatter_custom_fusion = f32[1025,128]{1,0:T(8,128)} fusion(s32[13312]{0:T(1024)} %bitcast.65, f32[13312,128]{1,0:T(8,128)} %reshape.231, f32[]{:T(128)} %constant.21.clone.1), kind=kCustom, calls=%fused_computation.33 | custom fusion | flops 1703936 | bytes 525312 | tf_op jit(solution)/shard_map/scatter-add | solution.py:58
  681.6 1.9 slice.60
  683.5 3.0 fusion.3
  686.6 66.6 %all-reduce.2 = f32[3456]{0:T(1024)S(1)} all-reduce(f32[3456]{0:T(1024)S(1)} %fusion.3), channel_id=5, replica_groups=mesh['dp'=32,'rep'=4] {'dp','rep'}, use_global_device_ids=true, to_apply=%region_14.15.clone | all-reduce | flops 3456 | bytes 27648
  753.7 1.6 multiply_reduce_fusion
  755.3 1.3 sqrt_add_fusion
  756.6 2.9 divide_subtract_fusion
  759.4 59.1 %all-reduce.9.cloned.1.call-done = (f32[512,3456]{1,0:T(8,128)}, f32[3456,512]{0,1:T(8,128)}) async-done(((f32[512,3456]{1,0:T(8,128)}, f32[3456,512]{0,1:T(8,128)}), (f32[512,3456]{1,0:T(8,128)}, f32[3456,512]{0,1:T(8,128)})) %all-reduce.9.cloned.1.call-update) | async-done | bytes 14155792
  820.5 1.5 constant_dynamic-slice_fusion.1
  822.1 163.3 %all-gather.3.cloned.1.call-done = f32[131072,128]{1,0:T(8,128)} async-done(((f32[1024,128]{1,0:T(8,128)}), f32[131072,128]{1,0:T(8,128)}) %all-gather.3.cloned.1.call-update) | async-done | bytes 67108880 | tf_op jit(solution)/shard_map/all_gather | solution.py:90
  985.4 21.8 %reduce_sum.45 = f32[1024,128]{1,0:T(8,128)} reduce(f32[128,1024,128]{2,1,0:T(8,128)} %bitcast.1, f32[]{:T(128)} %constant.21.clone.1), dimensions={0}, to_apply=%region_1.0 | reduce | flops 16646144 | bytes 67633152 | tf_op jit(solution)/shard_map/reduce_sum | solution.py:91
  1007.2 1.2 multiply_reduce_fusion.1
  1009.0 2.2 divide_subtract_fusion.1
  (49 shorter events, 12.1 us)
Async XLA Ops:
  7.2 362.8 %copy-start = (bf16[512,3456]{1,0:T(8,128)(2,1)S(1)}, bf16[512,3456]{1,0:T(8,128)(2,1)}, u32[]{:S(2)}) copy-start(bf16[512,3456]{1,0:T(8,128)(2,1)} %param.13) | copy-start | bytes 10616836
  16.4 0.6 copy-start.2
  353.9 147.7 %all-to-all-start = ((s32[32,1,208]{2,1,0:T(1,128)}), s32[32,1,208]{2,1,0:T(1,128)}, u32[]{:S(2)}, u32[]{:S(2)}) async-start(s32[32,1,208]{2,1,0:T(1,128)} %all_to_all.9), calls=%async_computation | async-start | bytes 65536 | tf_op jit(solution)/shard_map/all_to_all | solution.py:83
  363.7 3.1 copy-start.3
  363.7 4.1 copy-start.7
  367.9 2.1 copy-start.5
  370.0 2.3 copy-start.8
  372.2 4.2 copy-start.10
  374.3 2.2 copy-start.11
  497.4 95.8 %copy-start.4 = (bf16[512,3456]{1,0:T(8,128)(2,1)S(1)}, bf16[512,3456]{1,0:T(8,128)(2,1)}, u32[]{:S(2)}) copy-start(bf16[512,3456]{1,0:T(8,128)(2,1)} %param.10) | copy-start | bytes 10616836
  501.5 50.3 %all-to-all-start.1 = ((f32[32,208,128]{2,1,0:T(8,128)}), f32[32,208,128]{2,1,0:T(8,128)}, u32[]{:S(2)}, u32[]{:S(2)}) async-start(f32[32,208,128]{2,1,0:T(8,128)} %bitcast.57), calls=%async_computation.1 | async-start | bytes 6815744 | tf_op jit(solution)/shard_map/all_to_all | solution.py:82
  509.1 244.6 %all-reduce.7.cloned.1.call-start = ((), (), s32[]{:S(2)}) async-start(), calls=%async_computation.2 | async-start | bytes 2097152 | tf_op jit(solution)/shard_map/psum | solution.py:88
  593.1 225.5 %all-reduce.9.cloned.1.call-start = ((), (), s32[]{:S(2)}) async-start(), calls=%async_computation.4 | async-start | bytes 28311552
  593.2 6.2 copy-start.6
  593.2 6.2 copy-start.9
  604.4 381.0 %all-gather.3.cloned.1.call-start = ((), (), s32[]{:S(2)}) async-start(), calls=%async_computation.3 | async-start | bytes 67633152 | tf_op jit(solution)/shard_map/all_gather | solution.py:90
  985.4 23.1 %copy-start.12 = (f32[1024]{0:T(1024)S(1)}, f32[1024]{0:T(1024)}, u32[]{:S(2)}) copy-start(f32[1024]{0:T(1024)} %param.17) | copy-start | bytes 12292
  985.4 25.9 %copy-start.1 = (bf16[512,3456]{1,0:T(8,128)(2,1)S(1)}, bf16[512,3456]{1,0:T(8,128)(2,1)}, u32[]{:S(2)}) copy-start(bf16[512,3456]{1,0:T(8,128)(2,1)} %param.13) | copy-start | bytes 10616836
Sparse Core Ops, SparseCore 0:
  593.2 45.0 all-reduce.6
  644.2 174.3 all-reduce.8
  822.3 162.9 all-gather.2
